TPU v7x, 128 devices: a whole 4x4x4 slice. The times are simulated.
128 devices in a mesh: req: 4 (over z_lo, core), seq: 32 (over y, x, z_hi).
Axes of the slice: x: 4, y: 4, z: 4 (z_hi: 2, z_lo: 2; z = z_hi * 2 + z_lo), core: 2. Of those that a mesh axis runs over, the one named last changes fastest.
Arguments:
- prefill_query: bfloat16 [16384, 1536], P(('req', 'seq')), may hold values from -512 to 512
- prefill_key: bfloat16 [16384, 512], P(('req', 'seq')), may hold values from -512 to 512
- prefill_value: bfloat16 [16384, 512], P(('req', 'seq')), may hold values from -6 to 6
- prefill_resid: bfloat16 [16384, 1536], P(('req', 'seq')), may hold values from -6 to 6
- dec_query: bfloat16 [16, 1536], P('req'), may hold values from -512 to 512
- dec_key_new: bfloat16 [16, 512], P('req'), may hold values from -16 to 16
- dec_value_new: bfloat16 [16, 512], P('req'), may hold values from -6 to 6
- dec_resid: bfloat16 [16, 1536], P('req'), may hold values from -6 to 6
- cache_lengths: int32 [16], P('req'), may hold values from 16 to 32768, as said below
- key_cache: bfloat16 [16, 32768, 512], P('req', 'seq'), may hold values from -512 to 512
- value_cache: bfloat16 [16, 32768, 512], P('req', 'seq'), may hold values from -6 to 6
- attn_out_weight: bfloat16 [1536, 1536], replicated, may hold values from -0.15625 to 0.15625
- ffn_gain: float32 [1536], replicated, may hold values from 0.1 to 1.9
- expert_gate: bfloat16 [32, 1536, 512], P('seq', 'req'), may hold values from -0.15625 to 0.15625
- expert_up: bfloat16 [32, 1536, 512], P('seq', 'req'), may hold values from -0.15625 to 0.15625
- expert_down: bfloat16 [32, 512, 1536], P('seq', None, 'req'), may hold values from -0.25 to 0.25
- routes: int32 [16384, 8], P(('req', 'seq')), may hold values from 0 to 31, all different within a row; in each aligned block of 128 rows (0 to 127, 128 to 255, ...) at most 40 rows name the same one
- route_weights: float32 [16384, 8], P(('req', 'seq')), may hold values from 0.05 to 0.5
Outputs:
- prefill_out: bfloat16 [16384, 1536], P(('req', 'seq'))
- dec_out: bfloat16 [16, 1536], P('req')
Inputs may be any that keep to these rules, and one draw needn't show every extreme that they name: `routes`: in each aligned block of 128 rows (the rows of one device) no expert is named by more than 40 rows. `cache_lengths`: some request uses all 32768 positions.
All inputs are finite; a program needn't handle non-finite values.
Results may differ from a plain program's by a relative error of at most 0.012.
Values may be sent and summed in bfloat16 or wider, within the bound.
No kernel may reach another device: no remote copies, remote signals or barrier semaphores. Data moves between devices by JAX's collectives and lax.ppermute only.
A program may use at most 128 MiB of HBM per device.

v0:
```python
import math
import jax
import jax.numpy as jnp
from jax import lax
from jax.sharding import PartitionSpec as P

D = 1536
HEADS = 24
KVH = 8
HD = 64
EXPERTS = 32
CAP = 40
NEGATIVE = -1e30
EPSILON = 1e-05


def rms_scale(hidden, gain):
    values_float = hidden.astype(jnp.float32)
    mean_square = jnp.mean(values_float * values_float, axis=-1, keepdims=True)
    return (values_float * lax.rsqrt(mean_square + EPSILON) * gain).astype(jnp.bfloat16)


def per_request(function, operands):
    return jax.vmap(function)(operands)


def prefill_attention(prefill_query, prefill_key, prefill_value):
    token_rows = prefill_query.shape[0]
    group_size = HEADS // KVH
    score_scale = 1.0 / math.sqrt(HD)
    own_start = lax.axis_index("seq") * token_rows
    query_position = own_start + jnp.arange(token_rows, dtype=jnp.int32)
    query_heads = prefill_query.reshape(token_rows, KVH, group_size, HD)
    initial = (
        jnp.full((KVH, group_size, token_rows), NEGATIVE, jnp.float32),
        jnp.zeros((KVH, group_size, token_rows), jnp.float32),
        jnp.zeros((token_rows, KVH, group_size, HD), jnp.float32),
    )
    key_rows = lax.all_gather(prefill_key, "seq", axis=0, tiled=True)
    value_rows = lax.all_gather(prefill_value, "seq", axis=0, tiled=True)
    key_count = key_rows.shape[0]
    block_rows = 512
    key_heads = key_rows.reshape(key_count, KVH, HD)
    value_heads = value_rows.reshape(key_count, KVH, HD)

    def add_block(number, running_state):
        maxima, totals, weighted = running_state
        offset = number * block_rows
        key_block = lax.dynamic_slice_in_dim(key_heads, offset, block_rows, 0)
        value_block = lax.dynamic_slice_in_dim(value_heads, offset, block_rows, 0)
        key_position = offset + jnp.arange(block_rows, dtype=jnp.int32)
        visible = (key_position[None, :] <= query_position[:, None])[None, None, :, :]
        logits = (
            jnp.einsum("qkgd,pkd->kgqp", query_heads, key_block, preferred_element_type=jnp.float32)
            * score_scale
        )
        logits = jnp.where(visible, logits, NEGATIVE)
        new_maxima = jnp.maximum(maxima, jnp.max(logits, axis=-1))
        exponent = jnp.where(visible, jnp.exp(logits - new_maxima[..., None]), 0.0)
        rescale = jnp.exp(maxima - new_maxima)
        totals = totals * rescale + jnp.sum(exponent, axis=-1)
        weighted = weighted * jnp.moveaxis(rescale, 2, 0)[..., None] + jnp.einsum(
            "kgqp,pkd->qkgd",
            exponent.astype(jnp.bfloat16),
            value_block,
            preferred_element_type=jnp.float32,
        )
        return (new_maxima, totals, weighted)

    maxima, totals, weighted = lax.fori_loop(0, key_count // block_rows, add_block, initial)
    return (
        (weighted / jnp.moveaxis(totals, 2, 0)[..., None])
        .reshape(token_rows, HEADS * HD)
        .astype(jnp.bfloat16)
    )


def decode_attention(dec_query, dec_key_new, dec_value_new, cache_lengths, key_cache, value_cache):
    requests, block_length, feature_width = key_cache.shape
    group_size = HEADS // KVH
    score_scale = 1.0 / math.sqrt(HD)
    first_position = lax.axis_index("seq") * block_length
    positions = first_position + jnp.arange(block_length, dtype=jnp.int32)
    valid_mask = positions[None, :] < cache_lengths[:, None]
    query_heads = dec_query.reshape(requests, KVH, group_size, HD)
    key_heads = key_cache.reshape(requests, block_length, KVH, HD)
    value_heads = value_cache.reshape(requests, block_length, KVH, HD)

    def scores_of(pieces):
        query_one, keys_one, valid_one = pieces
        logits = (
            jnp.einsum("kgd,pkd->kgp", query_one, keys_one, preferred_element_type=jnp.float32)
            * score_scale
        )
        return jnp.where(valid_one[None, None, :], logits, NEGATIVE)

    def terms_of(pieces):
        scores_one, maxima_one, values_one, valid_one = pieces
        exponent = jnp.where(
            valid_one[None, None, :], jnp.exp(scores_one - maxima_one[..., None]), 0.0
        )
        weighted_one = jnp.einsum(
            "kgp,pkd->kgd",
            exponent.astype(jnp.bfloat16),
            values_one,
            preferred_element_type=jnp.float32,
        )
        return (jnp.sum(exponent, axis=-1), weighted_one)

    scores = per_request(scores_of, (query_heads, key_heads, valid_mask))
    local_maxima = jnp.max(scores, axis=-1)
    maxima = lax.pmax(local_maxima, "seq")
    totals, weighted = per_request(terms_of, (scores, maxima, value_heads, valid_mask))
    totals, weighted = lax.psum((totals, weighted), "seq")
    fresh_score = (
        jnp.einsum(
            "rkgd,rkd->rkg",
            query_heads,
            dec_key_new.reshape(requests, KVH, HD),
            preferred_element_type=jnp.float32,
        )
        * score_scale
    )
    final_maxima = jnp.maximum(maxima, fresh_score)
    rescale = jnp.exp(maxima - final_maxima)
    fresh_exp = jnp.exp(fresh_score - final_maxima)
    denominator = totals * rescale + fresh_exp
    fresh_weight = lax.optimization_barrier(fresh_exp.astype(jnp.bfloat16)).astype(jnp.float32)
    numerator = weighted * rescale[..., None] + fresh_weight[..., None] * dec_value_new.reshape(
        requests, KVH, 1, HD
    ).astype(jnp.float32)
    return (numerator / denominator[..., None]).reshape(requests, HEADS * HD).astype(jnp.bfloat16)


def expert_rows(rows_batch, gate_full, up_full, down_full):
    gate_value = jnp.einsum(
        "erd,edf->erf", rows_batch, gate_full, preferred_element_type=jnp.float32
    )
    up_value = jnp.einsum("erd,edf->erf", rows_batch, up_full, preferred_element_type=jnp.float32)
    hidden = (jax.nn.silu(gate_value) * up_value).astype(jnp.bfloat16)
    return jnp.einsum("erf,efd->erd", hidden, down_full, preferred_element_type=jnp.float32).astype(
        jnp.bfloat16
    )


def body(
    prefill_query,
    prefill_key,
    prefill_value,
    prefill_resid,
    dec_query,
    dec_key_new,
    dec_value_new,
    dec_resid,
    cache_lengths,
    key_cache,
    value_cache,
    attn_out_weight,
    ffn_gain,
    expert_gate,
    expert_up,
    expert_down,
    routes,
    route_weights,
):
    attended = prefill_attention(prefill_query, prefill_key, prefill_value)
    middle = (
        prefill_resid.astype(jnp.float32)
        + jnp.dot(attended, attn_out_weight, preferred_element_type=jnp.float32)
    ).astype(jnp.bfloat16)
    normed = rms_scale(middle, ffn_gain)
    gate_full, up_full = (
        lax.all_gather(expert_gate, "req", axis=1, tiled=True),
        lax.all_gather(expert_up, "req", axis=1, tiled=True),
    )
    down_full = lax.all_gather(expert_down, "req", axis=2, tiled=True)
    token_rows, top_count = routes.shape
    flat_expert = routes.reshape(-1)
    token_index = jnp.arange(token_rows * top_count, dtype=jnp.int32) // top_count
    onehot = (flat_expert[:, None] == jnp.arange(EXPERTS, dtype=jnp.int32)[None, :]).astype(
        jnp.int32
    )
    earlier = jnp.cumsum(onehot, axis=0) - onehot
    slot_index = jnp.sum(earlier * onehot, axis=1)
    outgoing = (
        jnp.zeros((EXPERTS, CAP, D), jnp.bfloat16)
        .at[flat_expert, slot_index]
        .set(normed[token_index])
    )
    incoming = lax.all_to_all(outgoing[:, None], "seq", split_axis=0, concat_axis=1, tiled=True)
    local_experts, sources, slot_count, feature_width = incoming.shape
    result = expert_rows(
        incoming.reshape(local_experts, sources * slot_count, feature_width),
        gate_full,
        up_full,
        down_full,
    )
    result = result.reshape(local_experts, sources, slot_count, feature_width)
    returned = lax.all_to_all(result, "seq", split_axis=1, concat_axis=0, tiled=True)
    picked = returned.reshape(EXPERTS, CAP, D)[flat_expert, slot_index]
    picked = picked.reshape(token_rows, top_count, D)
    mixture = jnp.sum(route_weights[..., None] * picked.astype(jnp.float32), axis=1)
    prefill_out = (middle.astype(jnp.float32) + mixture).astype(jnp.bfloat16)
    decoded = decode_attention(
        dec_query, dec_key_new, dec_value_new, cache_lengths, key_cache, value_cache
    )
    dec_out = (
        dec_resid.astype(jnp.float32)
        + jnp.dot(decoded, attn_out_weight, preferred_element_type=jnp.float32)
    ).astype(jnp.bfloat16)
    return (prefill_out, dec_out)


def solution(mesh):
    return jax.shard_map(
        body,
        mesh=mesh,
        in_specs=(
            P(("req", "seq"), None),
            P(("req", "seq"), None),
            P(("req", "seq"), None),
            P(("req", "seq"), None),
            P("req", None),
            P("req", None),
            P("req", None),
            P("req", None),
            P("req"),
            P("req", "seq", None),
            P("req", "seq", None),
            P(),
            P(),
            P("seq", "req", None),
            P("seq", "req", None),
            P("seq", None, "req"),
            P(("req", "seq"), None),
            P(("req", "seq"), None),
        ),
        out_specs=(P(("req", "seq"), None), P("req", None)),
        check_vma=False,
    )
```

profile of v0, /device:TPU:0, one launch (start us, length us, event | category | flops | bytes accessed | tf_op | source)
XLA Modules:
  0.0 821.3 jit_solution(3442623777327935929)
XLA Ops:
  12.3 9.0 %reduce-window.6 = s32[32,8,128]{2,1,0:T(8,128)S(1)} reduce-window(s32[32,8,128]{2,1,0:T(8,128)S(1)} %fusion.51, s32[]{:T(128)} %constant.93.clone.1), window={size=1x1x128 pad=0_0x0_0x127_0}, to_apply=%region_4.5 | reduce-window | flops 4161536 | bytes 262148 | tf_op jit(solution)/shard_map/reduce-window
  23.4 72.7 %all-gather.6.cloned.1.call-done = bf16[4096,512]{1,0:T(8,128)(2,1)} async-done(((bf16[128,512]{1,0:T(8,128)(2,1)}), bf16[4096,512]{1,0:T(8,128)(2,1)}) %all-gather.6.cloned.1.call-update) | async-done | bytes 4194320 | tf_op jit(solution)/shard_map/all_gather | solution.py:39
  96.1 6.4 copy.40
  102.5 75.9 %all-gather.8.cloned.1.call-done = bf16[4096,512]{1,0:T(8,128)(2,1)} async-done(((bf16[128,512]{1,0:T(8,128)(2,1)}), bf16[4096,512]{1,0:T(8,128)(2,1)}) %all-gather.8.cloned.1.call-update) | async-done | bytes 4194320 | tf_op jit(solution)/shard_map/all_gather | solution.py:40
  178.4 6.4 copy.42
  184.8 98.8 %while.18 = (s32[]{:T(128)}, f32[8,3,128]{2,1,0:T(4,128)S(1)}, f32[8,3,128]{2,1,0:T(4,128)S(1)}, f32[128,8,3,64]{0,3,2,1:T(8,128)S(1)}, bf16[4096,8,64]{0,2,1:T(...) while((s32[]{:T(128)}, f32[8,3,128]{2,1,0:T(4,128)S(1)}, ...), condition=%wide.region_3.4_spmd.clone, body=%wide.region_0.3_spmd.clone.sunk | while | flops 423774848 | bytes 47518944 | solution.py:70
  185.0 4.8 fusion.83
  197.5 4.8 fusion.83
  209.8 4.8 fusion.83
  222.2 4.8 fusion.83
  234.5 4.8 fusion.83
  246.8 4.8 fusion.83
  271.5 4.8 fusion.83
  288.0 18.6 %scatter_custom_fusion = bf16[1280,1536]{1,0:T(8,128)(2,1)} fusion(s32[1024]{0:T(1024)S(1)} %get-tuple-element.207, bf16[128,1536]{1,0:T(8,128)(2,1)S(1)} %multiply_convert_fusion, s32[1024]{0:T(1024)S(1)} %get-tuple-element.206, bf16[]{:T(256)} %constant.98.clone.1), kind=kCustom, calls=%fused_computation.36 | custom fusion | bytes 3932162
  306.7 5.1 all-to-all-start
  312.4 52.8 %all-to-all-done = bf16[32,1,40,1536]{3,2,1,0:T(8,128)(2,1)} async-done(((bf16[32,1,40,1536]{3,2,1,0:T(8,128)(2,1)}), bf16[32,1,40,1536]{3,2,1,0:T(8,128)(2,1)}, u32[]{:S(2)}, u32[]{:S(2)}) %all-to-all-start) | async-done | bytes 3932192 | tf_op jit(solution)/shard_map/all_to_all | solution.py:190
  365.2 4.8 fusion.36
  370.1 9.5 %convolution_convert_fusion = bf16[1280,1536]{1,0:T(8,128)(2,1)} fusion(bf16[1,512,1536]{2,1,0:T(8,128)(2,1)} %all-gather.14.cloned.1.call-done, bf16[1280,1536]{1,0:T(8,128)(2,1)} %bitcast.10, f32[1280,512]{1,0:T(8,128)S(1)} %fusion.36, bf16[1,1536,512]{2,1,0:T(8,128)(2,1)} %all-gather.12.cloned.1.call-done), kind=kOutput, calls=%fused_computation.32 | convolution fusion | flops 4032430080 | bytes 13631488 | tf_op jit(solution)/shard_map/erf,efd->erd/dot_general | solution.py:141
  379.5 7.5 all-to-all-start.1
  387.2 6.3 copy.51
  393.7 6.3 copy.50
  403.2 205.7 %pmax.7 = f32[4,8,3]{2,1,0:T(8,128)S(1)} all-reduce(f32[4,8,3]{2,1,0:T(8,128)S(1)} %get-tuple-element.204), channel_id=1, replica_groups=mesh['req'=4,'seq'=32] {'seq'}, use_global_device_ids=true, to_apply=%region_11.12 | all-reduce | flops 96 | bytes 768 | tf_op jit(solution)/shard_map/pmax | solution.py:112
  612.7 176.5 %all-reduce = (f32[4,8,3,64]{3,2,1,0:T(4,128)S(1)}, f32[4,8,3]{2,1,0:T(8,128)S(1)}) all-reduce(f32[4,8,3,64]{3,2,1,0:T(4,128)S(1)} %fusion.43, f32[4,8,3]{2,1,0:T(8,128)S(1)} %fusion.41), channel_id=1, replica_groups=mesh['req'=4,'seq'=32] {'seq'}, use_global_device_ids=true, to_apply=%region_12.13 | all-reduce | flops 6240 | bytes 49920 | tf_op jit(solution)/shard_map/psum | solution.py:114
  793.4 17.8 %gather_fusion = bf16[1024,1536]{1,0:T(8,128)(2,1)S(1)} fusion(bf16[32,40,1536]{2,1,0:T(8,128)(2,1)} %bitcast.16, s32[1024]{0:T(1024)S(1)} %bitcast.111), kind=kCustom, calls=%fused_computation.1 | custom fusion | bytes 6299648 | tf_op jit(solution)/shard_map/gather | solution.py:200
  (157 shorter events, 91.9 us)
Async XLA Ops:
  7.2 88.9 %all-gather.6.cloned.1.call-start = ((), (), s32[]{:S(2)}) async-start(), calls=%async_computation.2 | async-start | bytes 4325376 | tf_op jit(solution)/shard_map/all_gather | solution.py:39
  7.9 170.5 %all-gather.8.cloned.1.call-start = ((), (), s32[]{:S(2)}) async-start(), calls=%async_computation.3 | async-start | bytes 4325376 | tf_op jit(solution)/shard_map/all_gather | solution.py:40
  8.6 303.7 %all-gather.10.cloned.1.call-start = ((), (), s32[]{:S(2)}) async-start(), calls=%async_computation.4 | async-start | bytes 1966080 | tf_op jit(solution)/shard_map/all_gather | solution.py:173
  9.4 360.7 %all-gather.14.cloned.1.call-start = ((), (), s32[]{:S(2)}) async-start(), calls=%async_computation.6 | async-start | bytes 1966080 | tf_op jit(solution)/shard_map/all_gather | solution.py:176
  184.8 98.9 %copy-start.3 = (bf16[128,1536]{1,0:T(8,128)(2,1)S(1)}, bf16[128,1536]{1,0:T(8,128)(2,1)}, u32[]{:S(2)}) copy-start(bf16[128,1536]{1,0:T(8,128)(2,1)} %param.23) | copy-start | bytes 1179652
  189.8 4.7 copy-start
  202.3 4.6 copy-start
  214.6 4.6 copy-start
  227.0 4.6 copy-start
  239.3 4.6 copy-start
  251.6 4.6 copy-start
  263.9 4.6 copy-start
  276.2 4.6 copy-start
  283.6 4.3 copy-start.6
  306.7 58.5 %all-to-all-start = ((bf16[32,1,40,1536]{3,2,1,0:T(8,128)(2,1)}), bf16[32,1,40,1536]{3,2,1,0:T(8,128)(2,1)}, u32[]{:S(2)}, u32[]{:S(2)}) async-start(bf16[32,1,40,1536]{3,2,1,0:T(8,128)(2,1)} %bitcast.114), calls=%async_computation | async-start | bytes 7864320 | tf_op jit(solution)/shard_map/all_to_all | solution.py:190
  311.8 58.3 %all-gather.12.cloned.1.call-start = ((), (), s32[]{:S(2)}) async-start(), calls=%async_computation.5 | async-start | bytes 1966080 | tf_op jit(solution)/shard_map/all_gather | solution.py:174
  379.5 7.6 copy-start.7
  379.5 413.8 %all-to-all-start.1 = ((bf16[1,32,40,1536]{3,2,0,1:T(8,128)(2,1)}), bf16[1,32,40,1536]{3,2,0,1:T(8,128)(2,1)}, u32[]{:S(2)}, u32[]{:S(2)}) async-start(bf16[1,32,40,1536]{3,2,0,1:T(8,128)(2,1)} %bitcast.118), calls=%async_computation.1 | async-start | bytes 7864320 | tf_op jit(solution)/shard_map/all_to_all | solution.py:199
  387.2 6.3 copy-start.4
  393.6 6.4 copy-start.8
  393.6 6.4 copy-start.9
  393.7 6.5 copy-start.10
  403.2 386.5 %copy-start.5 = (bf16[4,1536]{1,0:T(4,128)(2,1)S(1)}, bf16[4,1536]{1,0:T(4,128)(2,1)}, u32[]{:S(2)}) copy-start(bf16[4,1536]{1,0:T(4,128)(2,1)} %param.27) | copy-start | bytes 36868
  811.2 2.8 copy-start.2
  (1 other events, 0.9 us)
Sparse Core Ops, SparseCore 0:
  11.0 85.0 all-gather.5
  99.1 79.3 all-gather.7
  180.1 21.5 all-gather.9
  203.2 25.7 all-gather.13
  313.9 54.2 all-gather.11
where the time goes:
time: 823 us; the launch traced here: 821 us
  blocking collectives  382 us (46%)
  waiting for transfers between devices  204 us (25%)
  matrix products  88 us (11%)
  local copies, waits for them, and re-layouts  67 us (8%)
  other arithmetic  52 us (6%)
  between operations  14.1 us (2%)
  starting transfers between devices  13 us (2%)
    pmax x1, blocking collectives, decode_attention(): maxima = lax.pmax(local_maxima, 'seq')  206 us
    psum x1, blocking collectives, decode_attention(): totals, weighted = lax.psum((totals, weighted), 'seq')  176 us
    all_gather x1, waiting for transfers between devices, prefill_attention(): value_rows = lax.all_gather(prefill_value, 'seq', axis=0, tiled=True)  75.9 us
    all_gather x1, waiting for transfers between devices, prefill_attention(): key_rows = lax.all_gather(prefill_key, 'seq', axis=0, tiled=True)  72.7 us
    all_to_all x1, waiting for transfers between devices, body(): lax.all_to_all(outgoing[:, None], 'seq', split_axis=0, concat_axis=1, til...  52.8 us
    dot_general x8, matrix products, add_block(): jnp.einsum('qkgd,pkd->kgqp', query_heads, key_block, preferred_element_ty...  38.2 us
    reduce_sum x8, other arithmetic, add_block(): totals = totals * rescale + jnp.sum(exponent, axis=-1)  35.4 us
    unnamed x26, local copies, waits for them, and re-layouts  34.3 us
  transfers between devices with their start and end apart: 7, of which 3 were waited for; matrix products, arithmetic and copies ran while one was open for 21% of the time, Pallas kernels for 0%

commit v1 on v0

--- a/solution.py
+++ b/solution.py
@@ -37,7 +37,9 @@
         jnp.zeros((token_rows, KVH, group_size, HD), jnp.float32),
     )
     key_rows = lax.all_gather(prefill_key, "seq", axis=0, tiled=True)
-    value_rows = lax.all_gather(prefill_value, "seq", axis=0, tiled=True)
+    value_rows = jnp.concatenate(
+        lax.all_to_all(jnp.stack([prefill_value] * lax.axis_size("seq")), "seq", 0, 0), axis=0
+    )
     key_count = key_rows.shape[0]
     block_rows = 512
     key_heads = key_rows.reshape(key_count, KVH, HD)

time: 823 us -> 780 us (0.948)
  waiting for transfers between devices: 204 us -> 139 us
  starting transfers between devices: 13 us -> 24 us
  local copies, waits for them, and re-layouts: 67 us -> 76.9 us
    all_gather x1 -> x0, waiting for transfers between devices: 75.9 us -> none  [prefill_attention(): value_rows = lax.all_gather(prefill_value, 'seq', axis=0, tiled=True)]
    all_to_all x0 -> x1, waiting for transfers between devices: none -> 48.9 us  [prefill_attention(): lax.all_to_all(jnp.stack([prefill_value] * lax.axis_size('seq')), 'seq',...]
    all_gather x1, waiting for transfers between devices: 72.7 us -> 34.9 us  [prefill_attention(): key_rows = lax.all_gather(prefill_key, 'seq', axis=0, tiled=True)]
    all_to_all x0 -> x1, starting transfers between devices: none -> 11 us  [prefill_attention(): lax.all_to_all(jnp.stack([prefill_value] * lax.axis_size('seq')), 'seq',...]
    another operation x2 -> x4, local copies, waits for them, and re-layouts: 0.08 us -> 10.3 us  [the longest x1 7.32 us: prefill_attention(): value_heads = value_rows.reshape(key_count, KVH, HD)]
    unnamed x26 -> x35, local copies, waits for them, and re-layouts: 34.3 us -> 33.7 us
  transfers between devices with their start and end apart: 7 -> 7, of which waited for: 3 -> 3; matrix products, arithmetic and copies ran while one was open for 21% -> 24% of each run, Pallas kernels for 0% -> 0%
where the time goes in v1:
time: 780 us; the launch traced here: 778 us
  blocking collectives  383 us (49%)
  waiting for transfers between devices  139 us (18%)
  matrix products  88.6 us (11%)
  local copies, waits for them, and re-layouts  76.9 us (10%)
  other arithmetic  51.1 us (7%)
  starting transfers between devices  24 us (3%)
  between operations  14.1 us (2%)
    pmax x1, blocking collectives, decode_attention(): maxima = lax.pmax(local_maxima, 'seq')  207 us
    psum x1, blocking collectives, decode_attention(): totals, weighted = lax.psum((totals, weighted), 'seq')  176 us
    all_to_all x1, waiting for transfers between devices, body(): lax.all_to_all(outgoing[:, None], 'seq', split_axis=0, concat_axis=1, til...  52.8 us
    all_to_all x1, waiting for transfers between devices, prefill_attention(): lax.all_to_all(jnp.stack([prefill_value] * lax.axis_size('seq')), 'seq',...  48.9 us
    dot_general x8, matrix products, add_block(): jnp.einsum('qkgd,pkd->kgqp', query_heads, key_block, preferred_element_ty...  38 us
    reduce_sum x8, other arithmetic, add_block(): totals = totals * rescale + jnp.sum(exponent, axis=-1)  35.6 us
    all_gather x1, waiting for transfers between devices, prefill_attention(): key_rows = lax.all_gather(prefill_key, 'seq', axis=0, tiled=True)  34.9 us
    unnamed x35, local copies, waits for them, and re-layouts  33.7 us
  transfers between devices with their start and end apart: 7, of which 3 were waited for; matrix products, arithmetic and copies ran while one was open for 24% of the time, Pallas kernels for 0%

profile of v1, /device:TPU:0, one launch (start us, length us, event | category | flops | bytes accessed | tf_op | source)
XLA Modules:
  0.0 777.6 jit_solution(10528343287864051817)
XLA Ops:
  11.8 11.0 %all-to-all-start = ((bf16[32,128,512]{1,2,0:T(8,128)(2,1)}), bf16[32,128,512]{1,2,0:T(8,128)(2,1)}, u32[]{:S(2)}, u32[]{:S(2)}) async-start(bf16[32,128,512]{1,2,0:T(8,128)(2,1)} %stack.2), calls=%async_computation | async-start | bytes 8388608 | tf_op jit(solution)/shard_map/all_to_all | solution.py:41
  25.0 9.0 %reduce-window.6 = s32[32,8,128]{2,1,0:T(8,128)S(1)} reduce-window(s32[32,8,128]{2,1,0:T(8,128)S(1)} %fusion.51, s32[]{:T(128)} %constant.93.clone.1), window={size=1x1x128 pad=0_0x0_0x127_0}, to_apply=%region_4.5 | reduce-window | flops 4161536 | bytes 262148 | tf_op jit(solution)/shard_map/reduce-window
  34.8 48.9 %all-to-all-done = bf16[32,128,512]{1,2,0:T(8,128)(2,1)} async-done(((bf16[32,128,512]{1,2,0:T(8,128)(2,1)}), bf16[32,128,512]{1,2,0:T(8,128)(2,1)}, u32[]{:S(2)}, u32[]{:S(2)}) %all-to-all-start) | async-done | bytes 4194336 | tf_op jit(solution)/shard_map/all_to_all | solution.py:41
  83.7 7.0 copy.56
  90.7 7.3 reshape_reshape.3
  98.0 34.9 %all-gather.5.cloned.1.call-done = bf16[4096,512]{1,0:T(8,128)(2,1)} async-done(((bf16[128,512]{1,0:T(8,128)(2,1)}), bf16[4096,512]{1,0:T(8,128)(2,1)}) %all-gather.5.cloned.1.call-update) | async-done | bytes 4194320 | tf_op jit(solution)/shard_map/all_gather | solution.py:39
  132.9 6.4 copy.53
  139.3 99.5 %while.18 = (s32[]{:T(128)}, f32[8,3,128]{2,1,0:T(4,128)S(1)}, f32[8,3,128]{2,1,0:T(4,128)S(1)}, f32[128,8,3,64]{0,3,2,1:T(8,128)S(1)}, bf16[4096,8,64]{0,2,1:T(...) while((s32[]{:T(128)}, f32[8,3,128]{2,1,0:T(4,128)S(1)}, ...), condition=%wide.region_3.4_spmd.clone, body=%wide.region_0.3_spmd.clone.sunk | while | flops 423774848 | bytes 47518944 | solution.py:72
  139.5 4.8 fusion.83
  152.0 4.8 fusion.83
  164.5 4.7 fusion.83
  176.9 4.8 fusion.83
  201.8 4.7 fusion.83
  243.2 18.6 %scatter_custom_fusion = bf16[1280,1536]{1,0:T(8,128)(2,1)} fusion(s32[1024]{0:T(1024)S(1)} %get-tuple-element.207, bf16[128,1536]{1,0:T(8,128)(2,1)S(1)} %multiply_convert_fusion, s32[1024]{0:T(1024)S(1)} %get-tuple-element.206, bf16[]{:T(256)} %constant.98.clone.1), kind=kCustom, calls=%fused_computation.36 | custom fusion | bytes 3932162
  261.9 5.1 all-to-all-start.1
  267.6 52.8 %all-to-all-done.1 = bf16[32,1,40,1536]{3,2,1,0:T(8,128)(2,1)} async-done(((bf16[32,1,40,1536]{3,2,1,0:T(8,128)(2,1)}), bf16[32,1,40,1536]{3,2,1,0:T(8,128)(2,1)}, u32[]{:S(2)}, u32[]{:S(2)}) %all-to-all-start.1) | async-done | bytes 3932192 | tf_op jit(solution)/shard_map/all_to_all | solution.py:192
  320.4 4.8 fusion.36
  325.3 9.4 %convolution_convert_fusion = bf16[1280,1536]{1,0:T(8,128)(2,1)} fusion(bf16[1,512,1536]{2,1,0:T(8,128)(2,1)} %all-gather.11.cloned.1.call-done, bf16[1280,1536]{1,0:T(8,128)(2,1)} %bitcast.9, f32[1280,512]{1,0:T(8,128)S(1)} %fusion.36, bf16[1,1536,512]{2,1,0:T(8,128)(2,1)} %all-gather.9.cloned.1.call-done), kind=kOutput, calls=%fused_computation.32 | convolution fusion | flops 4032430080 | bytes 13631488 | tf_op jit(solution)/shard_map/erf,efd->erd/dot_general | solution.py:143
  334.7 7.5 all-to-all-start.2
  342.4 6.3 copy.65
  348.8 6.3 copy.64
  358.3 206.8 %pmax.7 = f32[4,8,3]{2,1,0:T(8,128)S(1)} all-reduce(f32[4,8,3]{2,1,0:T(8,128)S(1)} %get-tuple-element.204), channel_id=1, replica_groups=mesh['req'=4,'seq'=32] {'seq'}, use_global_device_ids=true, to_apply=%region_11.12 | all-reduce | flops 96 | bytes 768 | tf_op jit(solution)/shard_map/pmax | solution.py:114
  568.9 176.5 %all-reduce = (f32[4,8,3,64]{3,2,1,0:T(4,128)S(1)}, f32[4,8,3]{2,1,0:T(8,128)S(1)}) all-reduce(f32[4,8,3,64]{3,2,1,0:T(4,128)S(1)} %fusion.43, f32[4,8,3]{2,1,0:T(8,128)S(1)} %fusion.41), channel_id=1, replica_groups=mesh['req'=4,'seq'=32] {'seq'}, use_global_device_ids=true, to_apply=%region_12.13 | all-reduce | flops 6240 | bytes 49920 | tf_op jit(solution)/shard_map/psum | solution.py:116
  749.6 17.8 %gather_fusion = bf16[1024,1536]{1,0:T(8,128)(2,1)S(1)} fusion(bf16[32,40,1536]{2,1,0:T(8,128)(2,1)} %bitcast.15, s32[1024]{0:T(1024)S(1)} %bitcast.112), kind=kCustom, calls=%fused_computation.1 | custom fusion | bytes 6299648 | tf_op jit(solution)/shard_map/gather | solution.py:202
  (167 shorter events, 102.6 us)
Async XLA Ops:
  7.2 125.7 %all-gather.5.cloned.1.call-start = ((), (), s32[]{:S(2)}) async-start(), calls=%async_computation.3 | async-start | bytes 4325376 | tf_op jit(solution)/shard_map/all_gather | solution.py:39
  11.8 12.5 %copy-start.8 = (s32[128,8]{0,1:T(8,128)S(1)}, s32[128,8]{0,1:T(8,128)}, u32[]{:S(2)}) copy-start(s32[128,8]{0,1:T(8,128)} %param.36) | copy-start | bytes 12292
  11.8 12.9 %copy-start.4 = (bf16[128,1536]{1,0:T(8,128)(2,1)S(1)}, bf16[128,1536]{1,0:T(8,128)(2,1)}, u32[]{:S(2)}) copy-start(bf16[128,1536]{1,0:T(8,128)(2,1)} %param.20) | copy-start | bytes 1179652
  11.8 22.8 %copy-start.14 = (s32[2]{0:T(128)S(1)}, s32[2]{0:T(128)}, u32[]{:S(2)}) copy-start(s32[2]{0:T(128)} %constant.114) | copy-start | bytes 28
  11.8 22.8 %copy-start.13 = (s32[2]{0:T(128)S(1)}, s32[2]{0:T(128)}, u32[]{:S(2)}) copy-start(s32[2]{0:T(128)} %constant.117) | copy-start | bytes 28
  11.8 71.9 %all-to-all-start = ((bf16[32,128,512]{1,2,0:T(8,128)(2,1)}), bf16[32,128,512]{1,2,0:T(8,128)(2,1)}, u32[]{:S(2)}, u32[]{:S(2)}) async-start(bf16[32,128,512]{1,2,0:T(8,128)(2,1)} %stack.2), calls=%async_computation | async-start | bytes 8388608 | tf_op jit(solution)/shard_map/all_to_all | solution.py:41
  22.8 244.7 %all-gather.7.cloned.1.call-start = ((), (), s32[]{:S(2)}) async-start(), calls=%async_computation.4 | async-start | bytes 1966080 | tf_op jit(solution)/shard_map/all_gather | solution.py:175
  23.6 301.7 %all-gather.11.cloned.1.call-start = ((), (), s32[]{:S(2)}) async-start(), calls=%async_computation.6 | async-start | bytes 1966080 | tf_op jit(solution)/shard_map/all_gather | solution.py:178
  139.3 99.6 %copy-start.3 = (bf16[128,1536]{1,0:T(8,128)(2,1)S(1)}, bf16[128,1536]{1,0:T(8,128)(2,1)}, u32[]{:S(2)}) copy-start(bf16[128,1536]{1,0:T(8,128)(2,1)} %param.23) | copy-start | bytes 1179652
  144.3 4.7 copy-start
  156.8 4.6 copy-start
  169.2 4.6 copy-start
  194.1 4.6 copy-start
  206.5 4.6 copy-start
  218.9 4.6 copy-start
  261.9 58.6 %all-to-all-start.1 = ((bf16[32,1,40,1536]{3,2,1,0:T(8,128)(2,1)}), bf16[32,1,40,1536]{3,2,1,0:T(8,128)(2,1)}, u32[]{:S(2)}, u32[]{:S(2)}) async-start(bf16[32,1,40,1536]{3,2,1,0:T(8,128)(2,1)} %bitcast.115), calls=%async_computation.1 | async-start | bytes 7864320 | tf_op jit(solution)/shard_map/all_to_all | solution.py:192
  267.0 58.3 %all-gather.9.cloned.1.call-start = ((), (), s32[]{:S(2)}) async-start(), calls=%async_computation.5 | async-start | bytes 1966080 | tf_op jit(solution)/shard_map/all_gather | solution.py:176
  334.7 7.6 copy-start.9
  334.7 414.9 %all-to-all-start.2 = ((bf16[1,32,40,1536]{3,2,0,1:T(8,128)(2,1)}), bf16[1,32,40,1536]{3,2,0,1:T(8,128)(2,1)}, u32[]{:S(2)}, u32[]{:S(2)}) async-start(bf16[1,32,40,1536]{3,2,0,1:T(8,128)(2,1)} %bitcast.118), calls=%async_computation.2 | async-start | bytes 7864320 | tf_op jit(solution)/shard_map/all_to_all | solution.py:201
  342.3 6.3 copy-start.5
  348.8 6.4 copy-start.10
  348.8 6.5 copy-start.11
  348.8 6.5 copy-start.12
  358.3 387.6 %copy-start.6 = (bf16[4,1536]{1,0:T(4,128)(2,1)S(1)}, bf16[4,1536]{1,0:T(4,128)(2,1)}, u32[]{:S(2)}) copy-start(bf16[4,1536]{1,0:T(4,128)(2,1)} %param.27) | copy-start | bytes 36868
  (5 other events, 17.3 us)
Sparse Core Ops, SparseCore 0:
  11.0 121.8 all-gather.4
  134.6 21.5 all-gather.6
  157.8 25.7 all-gather.10
  269.2 54.1 all-gather.8
